TPU v7x, 256 devices: a whole 4x4x8 slice. The times are simulated.
256 devices in a mesh: dp: 4 (over y), expert: 64 (over z, x, core).
Axes of the slice: x: 4, y: 4, z: 8, core: 2. Of those that a mesh axis runs over, the one named last changes fastest.
Arguments:
- tokens: bfloat16 [32768, 3584], P(('dp', 'expert')), may hold values from -6 to 6
- gate_up: bfloat16 [64, 3584, 2048], P('expert', 'dp'), may hold values from -0.09375 to 0.09375
- down_proj: bfloat16 [64, 1024, 3584], P('expert', None, 'dp'), may hold values from -0.1875 to 0.1875
- expert_ids: int32 [32768, 8], P(('dp', 'expert')), may hold values from 0 to 255, all different within a row; in each aligned block of 128 rows (0 to 127, 128 to 255, ...) at most 8 rows name the same one
- gate_weights: bfloat16 [32768, 8], P(('dp', 'expert')), may hold values from 0.049804688 to 1
Outputs:
- mixed: bfloat16 [32768, 3584], P(('dp', 'expert'))
Inputs may be any that keep to these rules, and one draw needn't show every extreme that they name: `expert_ids`: A row names 8 different experts. Among the rows of one device (aligned blocks of 128 rows), no expert is named by more than 8 rows.
All inputs are finite; a program needn't handle non-finite values.
Results may differ from a plain program's by a relative error of at most 0.0058.
Values may be sent and summed in bfloat16 or wider, within the bound.
A program may use at most 128 MiB of HBM per device.

v0:
```python
import jax
import jax.numpy as jnp
from jax import lax
from jax.sharding import PartitionSpec as P


def local(tokens, gate_up, down_proj, expert_ids, gate_weights):
    owners = lax.axis_size("expert")
    tok_rows = tokens.shape[0]
    width = tokens.shape[1]
    hidden_units = down_proj.shape[1]
    slots = 4 * tok_rows // owners
    total_rows = owners * slots
    owner_ids = jnp.arange(owners, dtype=jnp.int32)
    matches = expert_ids[:, :, None] == owner_ids[None, None, :]
    hits = jnp.sum(matches.astype(jnp.int32), axis=1)
    pick_weight = jnp.sum(
        jnp.where(matches, gate_weights[:, :, None].astype(jnp.float32), 0.0), axis=1
    )
    before = jnp.cumsum(hits, axis=0) - hits
    target = jnp.where(hits > 0, owner_ids[None, :] * slots + before, -1)
    slot_owner = jnp.arange(total_rows, dtype=jnp.int32) // slots
    slot_ids = jnp.arange(total_rows, dtype=jnp.int32)
    placed = jnp.take(target, slot_owner, axis=1) == slot_ids[None, :]
    place_bf = placed.astype(jnp.bfloat16)
    outgoing = jnp.dot(place_bf.T, tokens, preferred_element_type=jnp.float32).astype(jnp.bfloat16)
    arrived = lax.all_to_all(
        outgoing.reshape(owners, slots, width), "expert", split_axis=0, concat_axis=0, tiled=True
    )
    rows = arrived.reshape(total_rows, width)
    gu = jnp.dot(
        rows,
        lax.all_gather(gate_up, "dp", axis=1, tiled=True)[0],
        preferred_element_type=jnp.float32,
    )
    hidden = (jax.nn.silu(gu[:, :hidden_units]) * gu[:, hidden_units:]).astype(jnp.bfloat16)
    result = jnp.dot(
        hidden,
        lax.all_gather(down_proj, "dp", axis=2, tiled=True)[0],
        preferred_element_type=jnp.float32,
    ).astype(jnp.bfloat16)
    returned = lax.all_to_all(
        result.reshape(owners, slots, width), "expert", split_axis=0, concat_axis=0, tiled=True
    )
    weighted = (place_bf.astype(jnp.float32) * jnp.take(pick_weight, slot_owner, axis=1)).astype(
        jnp.bfloat16
    )
    mixed = jnp.dot(
        weighted, returned.reshape(total_rows, width), preferred_element_type=jnp.float32
    )
    return mixed.astype(jnp.bfloat16)


def solution(mesh):
    placed = (
        P(("dp", "expert"), None),
        P("expert", "dp", None),
        P("expert", None, "dp"),
        P(("dp", "expert"), None),
        P(("dp", "expert"), None),
    )
    return jax.shard_map(
        local, mesh=mesh, in_specs=placed, out_specs=P(("dp", "expert"), None), check_vma=False
    )
```

profile of v0, /device:TPU:1, one launch (start us, length us, event | category | flops | bytes accessed | tf_op | source)
XLA Modules:
  0.0 347.1 jit_solution(889905831543410198)
XLA Ops:
  6.5 0.0 copy-start
  6.5 0.0 copy-start.1
  6.5 0.0 all-gather.3.cloned.1.call-start
  6.5 0.7 all-gather.3.cloned.1.call-update
  7.3 0.0 all-gather.5.cloned.1.call-start
  7.3 0.7 all-gather.5.cloned.1.call-update
  8.0 0.0 copy-done.1
  8.1 0.1 copy.12
  8.2 0.2 reduce_window_sum.11
  8.4 0.1 copy.15
  8.5 1.0 gather_fusion
  9.5 0.1 bitcast_compare_fusion
  9.7 0.0 copy-done
  9.7 1.1 fusion.7
  10.8 96.9 %all_to_all.10 = bf16[64,8,3584]{2,1,0:T(8,128)(2,1)} all-to-all(bf16[64,8,3584]{2,1,0:T(8,128)(2,1)S(1)} %fusion.7), channel_id=1, replica_groups=mesh['dp'=4,'expert'=64] {'expert'}, dimensions={0} | all-to-all | bytes 7340032 | tf_op jit(solution)/shard_map/all_to_all | solution.py:27
  107.7 44.2 %all-gather.3.cloned.1.call-done = bf16[1,3584,2048]{2,1,0:T(8,128)(2,1)} async-done(((bf16[1,896,2048]{2,1,0:T(8,128)(2,1)}), bf16[1,3584,2048]{2,1,0:T(8,128)(2,1)}) %all-gather.3.cloned.1.call-update) | async-done | bytes 14680080 | tf_op jit(solution)/shard_map/all_gather | solution.py:33
  151.9 13.5 %fusion = f32[512,2048]{1,0:T(8,128)} fusion(bf16[1,3584,2048]{2,1,0:T(8,128)(2,1)} %all-gather.3.cloned.1.call-done, bf16[64,8,3584]{2,1,0:T(8,128)(2,1)} %all_to_all.10), kind=kOutput, calls=%fused_computation.2 | convolution fusion | flops 7516192768 | bytes 22544384 | tf_op jit(solution)/shard_map/dot_general | solution.py:31
  165.4 66.3 %all-gather.5.cloned.1.call-done = bf16[1,1024,3584]{2,1,0:T(8,128)(2,1)} async-done(((bf16[1,1024,896]{2,1,0:T(8,128)(2,1)}), bf16[1,1024,3584]{2,1,0:T(8,128)(2,1)}) %all-gather.5.cloned.1.call-update) | async-done | bytes 7340048 | tf_op jit(solution)/shard_map/all_gather | solution.py:39
  231.7 10.1 %fusion.8 = bf16[64,8,3584]{2,1,0:T(8,128)(2,1)} fusion(bf16[1,1024,3584]{2,1,0:T(8,128)(2,1)} %all-gather.5.cloned.1.call-done, f32[512,2048]{1,0:T(8,128)} %fusion), kind=kOutput, calls=%fused_computation.9 | convolution fusion | flops 3763077120 | bytes 15204352 | tf_op jit(solution)/shard_map/dot_general | solution.py:37
  241.9 11.0 %all-to-all-start.1 = ((bf16[64,8,3584]{2,1,0:T(8,128)(2,1)}), bf16[64,8,3584]{2,1,0:T(8,128)(2,1)}, u32[]{:S(2)}, u32[]{:S(2)}) async-start(bf16[64,8,3584]{2,1,0:T(8,128)(2,1)} %fusion.8), calls=%async_computation.1 | async-start | bytes 7340032 | tf_op jit(solution)/shard_map/all_to_all | solution.py:42
  252.8 0.0 copy-done.2
  252.9 1.0 gather_fusion.1
  253.9 82.6 %all-to-all-done.1 = bf16[64,8,3584]{2,1,0:T(8,128)(2,1)} async-done(((bf16[64,8,3584]{2,1,0:T(8,128)(2,1)}), bf16[64,8,3584]{2,1,0:T(8,128)(2,1)}, u32[]{:S(2)}, u32[]{:S(2)}) %all-to-all-start.1) | async-done | bytes 3670048 | tf_op jit(solution)/shard_map/all_to_all | solution.py:42
  336.6 3.7 %convolution_convert_fusion.1 = bf16[128,3584]{1,0:T(8,128)(2,1)} fusion(bf16[64,8,3584]{2,1,0:T(8,128)(2,1)} %all-to-all-done.1, f32[512,128]{1,0:T(8,128)S(1)} %gather_fusion.1, pred[128,512]{0,1:T(32,128)(4,1)S(1)} %bitcast_compare_fusion, pred[512]{0:T(512)(128)(4,1)S(1)} %compare_and_fusion), kind=kOutput, calls=%fused_computation.10 | convolution fusion | flops 470548480 | bytes 4915712 | tf_op jit(solution)/shard_map/dot_general | solution.py:48
  (9 shorter events, 0.1 us)
Async XLA Ops:
  6.5 3.1 copy-start
  6.5 1.5 copy-start.1
  6.5 145.4 %all-gather.3.cloned.1.call-start = ((), (), s32[]{:S(2)}) async-start(), calls=%async_computation.2 | async-start | bytes 18350080 | tf_op jit(solution)/shard_map/all_gather | solution.py:33
  7.3 224.5 %all-gather.5.cloned.1.call-start = ((), (), s32[]{:S(2)}) async-start(), calls=%async_computation.3 | async-start | bytes 9175040 | tf_op jit(solution)/shard_map/all_gather | solution.py:39
  241.9 11.0 %copy-start.2 = (bf16[128,8]{0,1:T(8,128)(2,1)S(1)}, bf16[128,8]{0,1:T(8,128)(2,1)}, u32[]{:S(2)}) copy-start(bf16[128,8]{0,1:T(8,128)(2,1)} %param.9) | copy-start | bytes 6148
  241.9 94.7 %all-to-all-start.1 = ((bf16[64,8,3584]{2,1,0:T(8,128)(2,1)}), bf16[64,8,3584]{2,1,0:T(8,128)(2,1)}, u32[]{:S(2)}, u32[]{:S(2)}) async-start(bf16[64,8,3584]{2,1,0:T(8,128)(2,1)} %fusion.8), calls=%async_computation.1 | async-start | bytes 7340032 | tf_op jit(solution)/shard_map/all_to_all | solution.py:42
Sparse Core Ops, SparseCore 0:
  9.2 142.6 all-gather.2
  153.7 77.9 all-gather.4
where the time goes:
time: 348 us; the launch traced here: 347 us
  waiting for transfers between devices  195 us (56%)
  blocking collectives  96.9 us (28%)
  matrix products  28.5 us (8%)
  between operations  13.5 us (4%)
  starting transfers between devices  11 us (3%)
    all_to_all x1, blocking collectives, local(): lax.all_to_all(outgoing.reshape(owners, slots, width), 'expert', split_ax...  96.9 us
    all_to_all x1, waiting for transfers between devices, local(): lax.all_to_all(result.reshape(owners, slots, width), 'expert', split_axis...  82.6 us
    all_gather x1, waiting for transfers between devices, local(): lax.all_gather(down_proj, 'dp', axis=2, tiled=True)[0]  66.3 us
    all_gather x1, waiting for transfers between devices, local(): lax.all_gather(gate_up, 'dp', axis=1, tiled=True)[0]  44.2 us
    dot_general x1, matrix products, local(): jnp.dot(rows, lax.all_gather(gate_up, 'dp', axis=1, tiled=True)[0], prefe...  13.5 us
    all_to_all x1, starting transfers between devices, local(): lax.all_to_all(result.reshape(owners, slots, width), 'expert', split_axis...  11 us
    dot_general x1, matrix products, local(): jnp.dot(hidden, lax.all_gather(down_proj, 'dp', axis=2, tiled=True)[0], p...  10.1 us
  transfers between devices with their start and end apart: 3, of which 3 were waited for; matrix products, arithmetic and copies ran while one was open for 5% of the time, Pallas kernels for 0%

commit v1 on v0

v1 whole, which is shorter than its diff:
```python
import functools

import jax
import jax.numpy as jnp
from jax import lax
from jax.experimental import pallas as pl
from jax.experimental.pallas import tpu as pltpu
from jax.sharding import PartitionSpec as P

MESH = pl.DeviceIdType.MESH
NZ, NX = 8, 4
SLOTS = 8
GROUPS = 4
DZ0 = (3, 4, 2, 1)
DZ1 = (5, 0, 6, 7)
GATE_CHUNKS = 7
DOWN_CHUNKS = 2


def kernel(
    tok_ref, gate_hbm, down_hbm, ids_ref, wts_ref, out_ref,
    place, comb, outgoing, rows, rows2, gate, down, acc, hidden, result, returned,
    disp_send, disp_recv, own_copy, gate_send, gate_in, gate_x, gate_sa, gate_sb,
    down_send, down_in, down_x, down_sa, down_sb, ret_send, ret_recv,
):
    p = lax.axis_index("dp")
    e = lax.axis_index("expert")
    z, x, c = e // 8, (e // 2) % 4, e % 2
    m = p // 2
    native = c == m
    foreign = c != m
    sibling = (p, e + 1 - 2 * c)
    pc = p + 1 - 2 * (p % 2)
    cross = (pc, e)
    across = (3 - p, e + 1 - 2 * c)
    home = jnp.where(native, p, 3 - p)
    ff = hidden.shape[1]
    depth = gate.shape[1]
    cols = down.shape[2]

    barrier = pltpu.get_barrier_semaphore()

    @pl.loop(0, 32)
    def _(i):
        ei = ((z + i // 4) % NZ * 4 + (x + i) % NX) * 2

        @pl.when((ei + m != e))
        def _():
            pl.semaphore_signal(barrier, inc=1, device_id=(p, ei + m), device_id_type=MESH)

        pl.semaphore_signal(barrier, inc=1, device_id=(3 - p, ei + m), device_id_type=MESH)
        pl.semaphore_signal(barrier, inc=1, device_id=(home, ei + 1 - m), device_id_type=MESH)

    pl.semaphore_signal(barrier, inc=1, device_id=cross, device_id_type=MESH)

    row = lax.broadcasted_iota(jnp.int32, (512, 128), 0)
    g, ii = row // 128, (row // 8) % 16
    zs, b, dx = ii % 2, (ii // 2) % 2, ii // 4
    dz0 = jnp.where(g == 0, DZ0[0], jnp.where(g == 1, DZ0[1], jnp.where(g == 2, DZ0[2], DZ0[3])))
    dz1 = jnp.where(g == 0, DZ1[0], jnp.where(g == 1, DZ1[1], jnp.where(g == 2, DZ1[2], DZ1[3])))
    dz = jnp.where(zs == 0, dz0, dz1)
    core = jnp.where(b == 0, m, 1 - m)
    expert = ((z + dz) % NZ * 4 + (x + dx) % NX) * 2 + core
    ids = ids_ref[...].T
    wts = wts_ref[...].astype(jnp.float32).T
    named = jnp.zeros((512, 128), jnp.float32)
    weight = jnp.zeros((512, 128), jnp.float32)
    for k in range(8):
        same = expert == ids[k : k + 1, :]
        named = jnp.where(same, 1.0, named)
        weight = jnp.where(same, wts[k : k + 1, :], weight)
    t0 = lax.broadcasted_iota(jnp.int32, (128, 128), 0)
    t1 = lax.broadcasted_iota(jnp.int32, (128, 128), 1)
    earlier = jnp.where(t0 < t1, 1.0, 0.0).astype(jnp.bfloat16)
    before = jnp.dot(named.astype(jnp.bfloat16), earlier, preferred_element_type=jnp.float32)
    slot = (row % 8).astype(jnp.float32)
    chosen = (named > 0.5) & (before == slot)
    place[...] = jnp.where(chosen, 1.0, 0.0).astype(jnp.bfloat16)
    comb[...] = jnp.where(chosen, weight, 0.0).T.astype(jnp.bfloat16)

    @pl.loop(0, 7)
    def _(n):
        at = pl.ds(pl.multiple_of(n * 512, 512), 512)
        block = jnp.dot(place[...], tok_ref[:, at], preferred_element_type=jnp.float32)
        outgoing[:, :, at] = block.astype(jnp.bfloat16).reshape(64, SLOTS, 512)

    pl.semaphore_wait(barrier, jnp.where(native, 96, 97))

    def remote(src, dst, ssem, rsem, to):
        return pltpu.make_async_remote_copy(
            src_ref=src, dst_ref=dst, send_sem=ssem, recv_sem=rsem, device_id=to, device_id_type=MESH
        )

    def piece(ref, k, i, size):
        return ref.at[k, pl.ds(i * size, size), :]

    gsize, dsize = depth // GATE_CHUNKS, ff // DOWN_CHUNKS

    def send_own(hbm, dst, size, chunks, ssem, arrive, to):
        @pl.loop(0, chunks)
        def _(i):
            remote(piece(hbm, 0, i, size), piece(dst, p, i, size), ssem, arrive.at[i], to).start()

    def forward(ref, k, i, size, ssem, arrive, to):
        remote(piece(ref, k, i, size), piece(ref, k, i, size), ssem, arrive.at[i], to).start()

    def arrived(ref, k, i, size, sem):
        pltpu.make_async_copy(piece(ref, k, i, size), piece(ref, k, i, size), sem.at[i]).wait()

    @pl.when(native)
    def _():
        send_own(gate_hbm, gate, gsize, GATE_CHUNKS, gate_send, gate_in, cross)
        send_own(gate_hbm, gate, gsize, GATE_CHUNKS, gate_send, gate_sa, sibling)
        pltpu.make_async_copy(gate_hbm.at[0], gate.at[p], own_copy.at[0]).start()
        pltpu.make_async_copy(down_hbm.at[0], down.at[p], own_copy.at[1]).start()

    @pl.when(foreign)
    def _():
        send_own(gate_hbm, gate, gsize, GATE_CHUNKS, gate_send, gate_in, across)

    for grp in range(GROUPS):

        @pl.loop(0, 16)
        def _(i, grp=grp):
            zsel, bb, ddx = i % 2, (i // 2) % 2, i // 4
            ddz = DZ0[grp] + (DZ1[grp] - DZ0[grp]) * zsel
            to = ((z + ddz) % NZ * 4 + (x + ddx) % NX) * 2 + m
            plane = p + bb * (3 - 2 * p)
            src = outgoing.at[grp * 16 + i]
            dst = rows.at[grp * 16 + i + 2 * (c - bb)]

            def go():
                remote(src, dst, disp_send, disp_recv.at[grp], (plane, to)).start()

            if grp == 1:
                own = native & (i == 1)

                @pl.when(own)
                def _():
                    pltpu.make_async_copy(src, dst, disp_recv.at[grp]).start()

                @pl.when(jnp.logical_not(own))
                def _():
                    go()
            else:
                go()

    @pl.when(native)
    def _():
        send_own(down_hbm, down, dsize, DOWN_CHUNKS, down_send, down_sa, sibling)

        @pl.loop(0, GATE_CHUNKS)
        def _(i):
            arrived(gate, pc, i, gsize, gate_in)
            forward(gate, pc, i, gsize, gate_send, gate_sb, sibling)

        send_own(down_hbm, down, dsize, DOWN_CHUNKS, down_send, down_in, cross)
        pltpu.make_async_copy(gate_hbm.at[0], gate.at[p], own_copy.at[0]).wait()
        pltpu.make_async_copy(down_hbm.at[0], down.at[p], own_copy.at[1]).wait()

    @pl.when(foreign)
    def _():
        @pl.loop(0, GATE_CHUNKS)
        def _(i):
            arrived(gate, 3 - p, i, gsize, gate_in)
            forward(gate, 3 - p, i, gsize, gate_send, gate_x, cross)
            forward(gate, 3 - p, i, gsize, gate_send, gate_sa, sibling)
            arrived(gate, 3 - pc, i, gsize, gate_x)
            forward(gate, 3 - pc, i, gsize, gate_send, gate_sb, sibling)

        send_own(down_hbm, down, dsize, DOWN_CHUNKS, down_send, down_in, across)

    for grp in range(GROUPS):
        part = rows.at[pl.ds(grp * 16, 16)]
        pltpu.make_async_copy(part, part, disp_recv.at[grp]).wait()

        @pl.loop(0, 7)
        def _(n, grp=grp):
            at = pl.ds(pl.multiple_of(n * 512, 512), 512)
            rows2[pl.ds(grp * 128, 128), at] = rows[pl.ds(grp * 16, 16), :, at].reshape(128, 512)

    def gate_part(k, first):
        @pl.loop(0, 8)
        def _(n):
            at = pl.ds(pl.multiple_of(n * 256, 256), 256)
            deep = pl.ds(pl.multiple_of(k * depth, 128), depth)
            part = jnp.dot(rows2[:, deep], gate[k, :, at], preferred_element_type=jnp.float32)
            if first:
                acc[:, at] = part
            else:
                acc[:, at] += part

    def sib_arrived(ref, k, size, chunks, sem):
        @pl.loop(0, chunks)
        def _(i):
            arrived(ref, k, i, size, sem)

    @pl.when(foreign)
    def _():
        sib_arrived(gate, p, gsize, GATE_CHUNKS, gate_sa)
        sib_arrived(gate, pc, gsize, GATE_CHUNKS, gate_sb)

    gate_part(p, True)
    gate_part(pc, False)

    @pl.when(native)
    def _():
        sib_arrived(gate, 3 - p, gsize, GATE_CHUNKS, gate_sa)
        sib_arrived(gate, 3 - pc, gsize, GATE_CHUNKS, gate_sb)

    gate_part(3 - p, False)
    gate_part(3 - pc, False)

    @pl.loop(0, ff // 256)
    def _(n):
        a = acc[:, pl.ds(pl.multiple_of(n * 256, 256), 256)]
        u = acc[:, pl.ds(pl.multiple_of(ff + n * 256, 256), 256)]
        hidden[:, pl.ds(pl.multiple_of(n * 256, 256), 256)] = (a / (1.0 + jnp.exp(-a)) * u).astype(jnp.bfloat16)

    def quarter(k):
        for half in range(2):
            part = jnp.dot(hidden[half * 256 : half * 256 + 256, :], down[k], preferred_element_type=jnp.float32)
            result[k, half * 32 : half * 32 + 32] = part.astype(jnp.bfloat16).reshape(32, SLOTS, cols)
            for grp in (2 * half, 2 * half + 1):

                @pl.loop(0, 16)
                def _(i, grp=grp):
                    zsel, cs, ddx = i % 2, (i // 2) % 2, i // 4
                    ddz = DZ0[grp] + (DZ1[grp] - DZ0[grp]) * zsel
                    to = ((z + NZ - ddz) % NZ * 4 + (x + NX - ddx) % NX) * 2 + cs
                    bb = jnp.where(native, 0, 1)
                    src = result.at[k, grp * 16 + i]
                    dst = returned.at[k, grp * 16 + i + 2 * (bb - cs)]

                    def go():
                        remote(src, dst, ret_send, ret_recv.at[k], (home, to)).start()

                    if grp == 1:
                        own = native & (zsel == 1) & (ddx == 0) & (cs == c)

                        @pl.when(own)
                        def _():
                            pltpu.make_async_copy(src, dst, ret_recv.at[k]).start()

                        @pl.when(jnp.logical_not(own))
                        def _():
                            go()
                    else:
                        go()

    @pl.when(foreign)
    def _():
        sib_arrived(down, p, dsize, DOWN_CHUNKS, down_sa)

    quarter(p)

    @pl.when(native)
    def _():
        @pl.loop(0, DOWN_CHUNKS)
        def _(i):
            arrived(down, pc, i, dsize, down_in)
            forward(down, pc, i, dsize, down_send, down_sb, sibling)

    @pl.when(foreign)
    def _():
        sib_arrived(down, pc, dsize, DOWN_CHUNKS, down_sb)

    quarter(pc)

    @pl.when(foreign)
    def _():
        @pl.loop(0, DOWN_CHUNKS)
        def _(i):
            arrived(down, 3 - p, i, dsize, down_in)
            forward(down, 3 - p, i, dsize, down_send, down_x, cross)
            forward(down, 3 - p, i, dsize, down_send, down_sa, sibling)

    @pl.when(native)
    def _():
        sib_arrived(down, 3 - p, dsize, DOWN_CHUNKS, down_sa)

    quarter(3 - p)

    @pl.when(foreign)
    def _():
        @pl.loop(0, DOWN_CHUNKS)
        def _(i):
            arrived(down, 3 - pc, i, dsize, down_x)
            forward(down, 3 - pc, i, dsize, down_send, down_sb, sibling)

    @pl.when(native)
    def _():
        sib_arrived(down, 3 - pc, dsize, DOWN_CHUNKS, down_sb)

    quarter(3 - pc)

    for k in range(4):
        pltpu.make_async_copy(returned.at[k], returned.at[k], ret_recv.at[k]).wait()
        mixed = jnp.dot(comb[...], returned[k].reshape(512, cols), preferred_element_type=jnp.float32)
        out_ref[:, k * cols : (k + 1) * cols] = mixed.astype(jnp.bfloat16)

    def sent(ref, sem):
        pltpu.make_async_copy(ref, ref, sem).wait()

    @pl.when(native)
    def _():
        sent(outgoing.at[pl.ds(0, 63)], disp_send)
        sent(gate.at[pl.ds(0, 3)], gate_send)
        sent(down.at[pl.ds(0, 3)], down_send)
        sent(result.at[pl.ds(0, 3)], ret_send)
        sent(result.at[3, pl.ds(0, 60)], ret_send)

    @pl.when(foreign)
    def _():
        sent(outgoing, disp_send)
        sent(gate, gate_send)
        sent(down, down_send)
        sent(result, ret_send)


def local(tokens, gate_up, down_proj, expert_ids, gate_weights):
    tok_rows, width = tokens.shape
    _, depth, wide = gate_up.shape
    _, ff, cols = down_proj.shape
    bf, f32 = jnp.bfloat16, jnp.float32
    vmem = pl.BlockSpec(memory_space=pltpu.VMEM)
    hbm = pl.BlockSpec(memory_space=pl.ANY)
    dma = pltpu.SemaphoreType.DMA
    return pl.pallas_call(
        kernel,
        out_shape=jax.ShapeDtypeStruct((tok_rows, width), bf),
        in_specs=[vmem, hbm, hbm, vmem, vmem],
        out_specs=vmem,
        scratch_shapes=[
            pltpu.VMEM((512, 128), bf),
            pltpu.VMEM((128, 512), bf),
            pltpu.VMEM((64, SLOTS, width), bf),
            pltpu.VMEM((64, SLOTS, width), bf),
            pltpu.VMEM((512, width), bf),
            pltpu.VMEM((4, depth, wide), bf),
            pltpu.VMEM((4, ff, cols), bf),
            pltpu.VMEM((512, wide), f32),
            pltpu.VMEM((512, ff), bf),
            pltpu.VMEM((4, 64, SLOTS, cols), bf),
            pltpu.VMEM((4, 64, SLOTS, cols), bf),
            dma, dma((GROUPS,)), dma((2,)),
            dma, dma((GATE_CHUNKS,)), dma((GATE_CHUNKS,)), dma((GATE_CHUNKS,)), dma((GATE_CHUNKS,)),
            dma, dma((DOWN_CHUNKS,)), dma((DOWN_CHUNKS,)), dma((DOWN_CHUNKS,)), dma((DOWN_CHUNKS,)),
            dma, dma((4,)),
        ],
        compiler_params=pltpu.CompilerParams(
            collective_id=0, has_side_effects=True, vmem_limit_bytes=60 * 1024 * 1024
        ),
    )(tokens, gate_up, down_proj, expert_ids, gate_weights)


def solution(mesh):
    placed = (
        P(("dp", "expert"), None),
        P("expert", "dp", None),
        P("expert", None, "dp"),
        P(("dp", "expert"), None),
        P(("dp", "expert"), None),
    )
    return jax.shard_map(
        local, mesh=mesh, in_specs=placed, out_specs=P(("dp", "expert"), None), check_vma=False
    )
```

time: 348 us -> 219 us (0.63)
  Pallas kernels: 0 us -> 214 us
  waiting for transfers between devices: 195 us -> 0 us
  blocking collectives: 96.9 us -> 0 us
  matrix products: 28.5 us -> 0 us
  between operations: 13.5 us -> 0.01 us
  starting transfers between devices: 11 us -> 0 us
    pallas_call x0 -> x1, Pallas kernels: none -> 214 us  [local(): pl.pallas_call(kernel, out_shape=jax.ShapeDtypeStruct((tok_rows, width),...]
    all_gather x2 -> x0, waiting for transfers between devices: 111 us -> none  [the longest x1 66.3 us: local(): lax.all_gather(down_proj, 'dp', axis=2, tiled=True)[0]]
    all_to_all x1 -> x0, blocking collectives: 96.9 us -> none  [local(): lax.all_to_all(outgoing.reshape(owners, slots, width), 'expert', split_ax...]
    all_to_all x1 -> x0, waiting for transfers between devices: 82.6 us -> none  [local(): lax.all_to_all(result.reshape(owners, slots, width), 'expert', split_axis...]
    dot_general x4 -> x0, matrix products: 28.5 us -> none  [the longest x1 13.5 us: local(): jnp.dot(rows, lax.all_gather(gate_up, 'dp', axis=1, tiled=True)[0], prefe...]
    all_to_all x1 -> x0, starting transfers between devices: 11 us -> none  [local(): lax.all_to_all(result.reshape(owners, slots, width), 'expert', split_axis...]
    unnamed x6 -> x3, local copies, waits for them, and re-layouts: 0.01 us -> 4.96 us
  transfers between devices with their start and end apart: 3 -> 0, of which waited for: 3 -> 0; matrix products, arithmetic and copies ran while one was open for 5% -> 0% of each run, Pallas kernels for 0% -> 0%
where the time goes in v1:
time: 219 us
  Pallas kernels  214 us (98%)
  local copies, waits for them, and re-layouts  4.96 us (2%)
    pallas_call x1, Pallas kernels, local(): pl.pallas_call(kernel, out_shape=jax.ShapeDtypeStruct((tok_rows, width),...  214 us
    unnamed x3, local copies, waits for them, and re-layouts  4.96 us

profile of v1, /device:TPU:1, one launch (start us, length us, event | category | flops | bytes accessed | tf_op | source)
XLA Modules:
  0.0 218.6 jit_solution(12483924298821679826)
XLA Ops:
  0.0 1.4 copy.7.wts_ref
  1.4 1.4 copy.6.ids_ref
  2.8 213.6 %shard_map.55 = bf16[128,3584]{1,0:T(8,128)(2,1)} custom-call(bf16[128,3584]{1,0:T(8,128)(2,1)} %tok_ref.1, bf16[1,896,2048]{2,1,0:T(8,128)(2,1)} %gate_hbm.1, bf16[1,1024,896]{2,1,0:T(8,128)(2,1)} %down_hbm.1, s32[128,8]{1,0:T(8,128)} %copy.6.ids_ref, bf16[128,8]{1,0:T(8,128)(2,1)} %copy.7.wts_ref), custom_call_target="tpu_custom_call" | custom-call | tf_op jit(solution)/shard_map/pallas_call | solution.py:329
  216.4 2.2 copy.9

commit v2 on v1

--- a/solution.py
+++ b/solution.py
@@ -14,7 +14,7 @@
 DZ0 = (3, 4, 2, 1)
 DZ1 = (5, 0, 6, 7)
 GATE_CHUNKS = 7
-DOWN_CHUNKS = 2
+DOWN_CHUNKS = 4
 
 
 def kernel(
@@ -40,18 +40,21 @@
 
     barrier = pltpu.get_barrier_semaphore()
 
-    @pl.loop(0, 32)
-    def _(i):
-        ei = ((z + i // 4) % NZ * 4 + (x + i) % NX) * 2
-
-        @pl.when((ei + m != e))
-        def _():
-            pl.semaphore_signal(barrier, inc=1, device_id=(p, ei + m), device_id_type=MESH)
-
-        pl.semaphore_signal(barrier, inc=1, device_id=(3 - p, ei + m), device_id_type=MESH)
-        pl.semaphore_signal(barrier, inc=1, device_id=(home, ei + 1 - m), device_id_type=MESH)
-
-    pl.semaphore_signal(barrier, inc=1, device_id=cross, device_id_type=MESH)
+    def greet(plane, to):
+        pl.semaphore_signal(barrier, inc=1, device_id=(plane, to), device_id_type=MESH)
+
+    for ddz in (4, 3, 5, 2, 6, 1, 7, 0):
+        for ddx in (2, 1, 3, 0):
+            chip = ((z + ddz) % NZ * 4 + (x + ddx) % NX) * 2
+            greet(3 - p, chip + m)
+            greet(home, chip + 1 - m)
+            if ddz or ddx:
+                greet(p, chip + m)
+    greet(*cross)
+
+    @pl.when(foreign)
+    def _():
+        greet(*sibling)
 
     row = lax.broadcasted_iota(jnp.int32, (512, 128), 0)
     g, ii = row // 128, (row // 8) % 16
@@ -149,76 +152,102 @@
     def _():
         send_own(down_hbm, down, dsize, DOWN_CHUNKS, down_send, down_sa, sibling)
 
-        @pl.loop(0, GATE_CHUNKS)
-        def _(i):
+    def pass_on(i):
+        @pl.when(native)
+        def _():
             arrived(gate, pc, i, gsize, gate_in)
             forward(gate, pc, i, gsize, gate_send, gate_sb, sibling)
 
-        send_own(down_hbm, down, dsize, DOWN_CHUNKS, down_send, down_in, cross)
-        pltpu.make_async_copy(gate_hbm.at[0], gate.at[p], own_copy.at[0]).wait()
-        pltpu.make_async_copy(down_hbm.at[0], down.at[p], own_copy.at[1]).wait()
-
-    @pl.when(foreign)
-    def _():
-        @pl.loop(0, GATE_CHUNKS)
-        def _(i):
+        @pl.when(foreign)
+        def _():
             arrived(gate, 3 - p, i, gsize, gate_in)
             forward(gate, 3 - p, i, gsize, gate_send, gate_x, cross)
             forward(gate, 3 - p, i, gsize, gate_send, gate_sa, sibling)
             arrived(gate, 3 - pc, i, gsize, gate_x)
             forward(gate, 3 - pc, i, gsize, gate_send, gate_sb, sibling)
 
-        send_own(down_hbm, down, dsize, DOWN_CHUNKS, down_send, down_in, across)
-
-    for grp in range(GROUPS):
+    def from_sibling(ref, k, size, chunks, sem):
+        for i in chunks:
+            arrived(ref, k, i, size, sem)
+
+    def rows_in(grp):
         part = rows.at[pl.ds(grp * 16, 16)]
         pltpu.make_async_copy(part, part, disp_recv.at[grp]).wait()
 
         @pl.loop(0, 7)
-        def _(n, grp=grp):
+        def _(n):
             at = pl.ds(pl.multiple_of(n * 512, 512), 512)
-            rows2[pl.ds(grp * 128, 128), at] = rows[pl.ds(grp * 16, 16), :, at].reshape(128, 512)
-
-    def gate_part(k, first):
-        @pl.loop(0, 8)
+            rows2[grp * 128 : grp * 128 + 128, at] = rows[grp * 16 : grp * 16 + 16, :, at].reshape(128, 512)
+
+    def gate_sum(parts, r, at):
+        total = None
+        for k, k0, kd in parts:
+            deep = pl.ds(pl.multiple_of(k * depth + k0, 128), kd)
+            term = jnp.dot(rows2[r, deep], gate[k, k0 : k0 + kd, at], preferred_element_type=jnp.float32)
+            total = term if total is None else total + term
+        return total
+
+    def gate_begin(parts, r):
+        @pl.loop(0, 2 * ff // 256)
         def _(n):
             at = pl.ds(pl.multiple_of(n * 256, 256), 256)
-            deep = pl.ds(pl.multiple_of(k * depth, 128), depth)
-            part = jnp.dot(rows2[:, deep], gate[k, :, at], preferred_element_type=jnp.float32)
-            if first:
-                acc[:, at] = part
-            else:
-                acc[:, at] += part
-
-    def sib_arrived(ref, k, size, chunks, sem):
-        @pl.loop(0, chunks)
-        def _(i):
-            arrived(ref, k, i, size, sem)
-
-    @pl.when(foreign)
-    def _():
-        sib_arrived(gate, p, gsize, GATE_CHUNKS, gate_sa)
-        sib_arrived(gate, pc, gsize, GATE_CHUNKS, gate_sb)
-
-    gate_part(p, True)
-    gate_part(pc, False)
-
-    @pl.when(native)
-    def _():
-        sib_arrived(gate, 3 - p, gsize, GATE_CHUNKS, gate_sa)
-        sib_arrived(gate, 3 - pc, gsize, GATE_CHUNKS, gate_sb)
-
-    gate_part(3 - p, False)
-    gate_part(3 - pc, False)
-
-    @pl.loop(0, ff // 256)
-    def _(n):
-        a = acc[:, pl.ds(pl.multiple_of(n * 256, 256), 256)]
-        u = acc[:, pl.ds(pl.multiple_of(ff + n * 256, 256), 256)]
-        hidden[:, pl.ds(pl.multiple_of(n * 256, 256), 256)] = (a / (1.0 + jnp.exp(-a)) * u).astype(jnp.bfloat16)
-
-    def quarter(k):
-        for half in range(2):
+            acc[r, at] = gate_sum(parts, r, at)
+
+    def gate_finish(parts, r, begun):
+        @pl.loop(0, ff // 256)
+        def _(n):
+            at = pl.ds(pl.multiple_of(n * 256, 256), 256)
+            up = pl.ds(pl.multiple_of(ff + n * 256, 256), 256)
+            a, u = gate_sum(parts, r, at), gate_sum(parts, r, up)
+            if begun:
+                a, u = a + acc[r, at], u + acc[r, up]
+            hidden[r, at] = (a / (1.0 + jnp.exp(-a)) * u).astype(jnp.bfloat16)
+
+    early = 5
+    cut = early * gsize
+    first = [(p, 0, depth), (pc, 0, cut), (3 - p, 0, cut), (3 - pc, 0, cut)]
+    last = [(k, cut, depth - cut) for k in (pc, 3 - p, 3 - pc)]
+    whole = [(k, 0, depth) for k in (p, pc, 3 - p, 3 - pc)]
+
+    for i in range(early):
+        pass_on(i)
+
+    @pl.when(native)
+    def _():
+        pltpu.make_async_copy(gate_hbm.at[0], gate.at[p], own_copy.at[0]).wait()
+        pltpu.make_async_copy(down_hbm.at[0], down.at[p], own_copy.at[1]).wait()
+        from_sibling(gate, 3 - p, gsize, range(early), gate_sa)
+        from_sibling(gate, 3 - pc, gsize, range(early), gate_sb)
+
+    @pl.when(foreign)
+    def _():
+        from_sibling(gate, p, gsize, range(GATE_CHUNKS), gate_sa)
+        from_sibling(gate, pc, gsize, range(early), gate_sb)
+
+    rows_in(0)
+    rows_in(1)
+    gate_begin(first, slice(0, 256))
+    pass_on(early)
+    rows_in(2)
+    gate_begin(first, slice(256, 384))
+    for i in range(early + 1, GATE_CHUNKS):
+        pass_on(i)
+
+    @pl.when(native)
+    def _():
+        send_own(down_hbm, down, dsize, DOWN_CHUNKS, down_send, down_in, cross)
+        from_sibling(gate, 3 - p, gsize, range(early, GATE_CHUNKS), gate_sa)
+        from_sibling(gate, 3 - pc, gsize, range(early, GATE_CHUNKS), gate_sb)
+
+    @pl.when(foreign)
+    def _():
+        send_own(down_hbm, down, dsize, DOWN_CHUNKS, down_send, down_in, across)
+        from_sibling(gate, pc, gsize, range(early, GATE_CHUNKS), gate_sb)
+
+    gate_finish(last, slice(0, 384), True)
+
+    def quarter(k, halves):
+        for half in halves:
             part = jnp.dot(hidden[half * 256 : half * 256 + 256, :], down[k], preferred_element_type=jnp.float32)
             result[k, half * 32 : half * 32 + 32] = part.astype(jnp.bfloat16).reshape(32, SLOTS, cols)
             for grp in (2 * half, 2 * half + 1):
@@ -250,49 +279,49 @@
 
     @pl.when(foreign)
     def _():
-        sib_arrived(down, p, dsize, DOWN_CHUNKS, down_sa)
-
-    quarter(p)
-
-    @pl.when(native)
-    def _():
-        @pl.loop(0, DOWN_CHUNKS)
-        def _(i):
+        from_sibling(down, p, dsize, range(DOWN_CHUNKS), down_sa)
+
+    quarter(p, (0,))
+    rows_in(3)
+    gate_finish(whole, slice(384, 512), False)
+    quarter(p, (1,))
+
+    @pl.when(native)
+    def _():
+        for i in range(DOWN_CHUNKS):
             arrived(down, pc, i, dsize, down_in)
             forward(down, pc, i, dsize, down_send, down_sb, sibling)
 
     @pl.when(foreign)
     def _():
-        sib_arrived(down, pc, dsize, DOWN_CHUNKS, down_sb)
-
-    quarter(pc)
-
-    @pl.when(foreign)
-    def _():
-        @pl.loop(0, DOWN_CHUNKS)
-        def _(i):
+        for i in range(DOWN_CHUNKS):
             arrived(down, 3 - p, i, dsize, down_in)
             forward(down, 3 - p, i, dsize, down_send, down_x, cross)
             forward(down, 3 - p, i, dsize, down_send, down_sa, sibling)
 
-    @pl.when(native)
-    def _():
-        sib_arrived(down, 3 - p, dsize, DOWN_CHUNKS, down_sa)
-
-    quarter(3 - p)
-
-    @pl.when(foreign)
-    def _():
-        @pl.loop(0, DOWN_CHUNKS)
-        def _(i):
+    quarter(jnp.where(native, pc, 3 - p), (0, 1))
+
+    @pl.when(native)
+    def _():
+        from_sibling(down, 3 - p, dsize, range(DOWN_CHUNKS), down_sa)
+
+    @pl.when(foreign)
+    def _():
+        from_sibling(down, pc, dsize, range(DOWN_CHUNKS), down_sb)
+
+    quarter(jnp.where(native, 3 - p, pc), (0, 1))
+
+    @pl.when(foreign)
+    def _():
+        for i in range(DOWN_CHUNKS):
             arrived(down, 3 - pc, i, dsize, down_x)
             forward(down, 3 - pc, i, dsize, down_send, down_sb, sibling)
 
     @pl.when(native)
     def _():
-        sib_arrived(down, 3 - pc, dsize, DOWN_CHUNKS, down_sb)
-
-    quarter(3 - pc)
+        from_sibling(down, 3 - pc, dsize, range(DOWN_CHUNKS), down_sb)
+
+    quarter(3 - pc, (0, 1))
 
     for k in range(4):
         pltpu.make_async_copy(returned.at[k], returned.at[k], ret_recv.at[k]).wait()

time: 219 us -> 212 us (0.968)
  Pallas kernels: 214 us -> 207 us
    pallas_call x1, Pallas kernels: 214 us -> 207 us  [local(): pl.pallas_call(kernel, out_shape=jax.ShapeDtypeStruct((tok_rows, width),...]
where the time goes in v2:
time: 212 us
  Pallas kernels  207 us (98%)
  local copies, waits for them, and re-layouts  4.96 us (2%)
    pallas_call x1, Pallas kernels, local(): pl.pallas_call(kernel, out_shape=jax.ShapeDtypeStruct((tok_rows, width),...  207 us
    unnamed x3, local copies, waits for them, and re-layouts  4.96 us

profile of v2, /device:TPU:1, one launch (start us, length us, event | category | flops | bytes accessed | tf_op | source)
XLA Modules:
  0.0 211.5 jit_solution(5166335395716281528)
XLA Ops:
  0.0 1.4 copy.7.wts_ref
  1.4 1.4 copy.6.ids_ref
  2.8 206.6 %shard_map.55 = bf16[128,3584]{1,0:T(8,128)(2,1)} custom-call(bf16[128,3584]{1,0:T(8,128)(2,1)} %tok_ref.1, bf16[1,896,2048]{2,1,0:T(8,128)(2,1)} %gate_hbm.1, bf16[1,1024,896]{2,1,0:T(8,128)(2,1)} %down_hbm.1, s32[128,8]{1,0:T(8,128)} %copy.6.ids_ref, bf16[128,8]{1,0:T(8,128)(2,1)} %copy.7.wts_ref), custom_call_target="tpu_custom_call" | custom-call | tf_op jit(solution)/shard_map/pallas_call | solution.py:358
  209.4 2.2 %copy.9 = bf16[128,3584]{1,0:T(8,128)(2,1)} copy(bf16[128,3584]{1,0:T(8,128)(2,1)} %shard_map.55) | data formatting | bytes 1835008

commit v3 on v2

--- a/solution.py
+++ b/solution.py
@@ -15,6 +15,9 @@
 DZ1 = (5, 0, 6, 7)
 GATE_CHUNKS = 7
 DOWN_CHUNKS = 4
+AHEAD = 7
+LAG = 1
+DISPATCH = ((0,), (1,), (), (2,), (3,), (), (), ())
 
 
 def kernel(
@@ -100,8 +103,7 @@
     gsize, dsize = depth // GATE_CHUNKS, ff // DOWN_CHUNKS
 
     def send_own(hbm, dst, size, chunks, ssem, arrive, to):
-        @pl.loop(0, chunks)
-        def _(i):
+        for i in chunks:
             remote(piece(hbm, 0, i, size), piece(dst, p, i, size), ssem, arrive.at[i], to).start()
 
     def forward(ref, k, i, size, ssem, arrive, to):
@@ -110,21 +112,21 @@
     def arrived(ref, k, i, size, sem):
         pltpu.make_async_copy(piece(ref, k, i, size), piece(ref, k, i, size), sem.at[i]).wait()
 
-    @pl.when(native)
-    def _():
-        send_own(gate_hbm, gate, gsize, GATE_CHUNKS, gate_send, gate_in, cross)
-        send_own(gate_hbm, gate, gsize, GATE_CHUNKS, gate_send, gate_sa, sibling)
-        pltpu.make_async_copy(gate_hbm.at[0], gate.at[p], own_copy.at[0]).start()
-        pltpu.make_async_copy(down_hbm.at[0], down.at[p], own_copy.at[1]).start()
-
-    @pl.when(foreign)
-    def _():
-        send_own(gate_hbm, gate, gsize, GATE_CHUNKS, gate_send, gate_in, across)
-
-    for grp in range(GROUPS):
-
+    def send_gate(chunks):
+        @pl.when(native)
+        def _():
+            send_own(gate_hbm, gate, gsize, chunks, gate_send, gate_in, cross)
+            send_own(gate_hbm, gate, gsize, chunks, gate_send, gate_sa, sibling)
+
+        @pl.when(foreign)
+        def _():
+            send_own(gate_hbm, gate, gsize, chunks, gate_send, gate_in, across)
+
+    send_gate(range(AHEAD))
+
+    def dispatch(grp):
         @pl.loop(0, 16)
-        def _(i, grp=grp):
+        def _(i):
             zsel, bb, ddx = i % 2, (i // 2) % 2, i // 4
             ddz = DZ0[grp] + (DZ1[grp] - DZ0[grp]) * zsel
             to = ((z + ddz) % NZ * 4 + (x + ddx) % NX) * 2 + m
@@ -148,11 +150,23 @@
             else:
                 go()
 
-    @pl.when(native)
-    def _():
-        send_own(down_hbm, down, dsize, DOWN_CHUNKS, down_send, down_sa, sibling)
+    for grp in DISPATCH[0]:
+        dispatch(grp)
+
+    @pl.when(native)
+    def _():
+        pltpu.make_async_copy(gate_hbm.at[0], gate.at[p], own_copy.at[0]).start()
+        pltpu.make_async_copy(down_hbm.at[0], down.at[p], own_copy.at[1]).start()
+        send_own(down_hbm, down, dsize, range(DOWN_CHUNKS), down_send, down_sa, sibling)
+
+    def share_far(i):
+        arrived(gate, 3 - pc, i, gsize, gate_x)
+        forward(gate, 3 - pc, i, gsize, gate_send, gate_sb, sibling)
 
     def pass_on(i):
+        if i + AHEAD < GATE_CHUNKS:
+            send_gate([i + AHEAD])
+
         @pl.when(native)
         def _():
             arrived(gate, pc, i, gsize, gate_in)
@@ -163,8 +177,20 @@
             arrived(gate, 3 - p, i, gsize, gate_in)
             forward(gate, 3 - p, i, gsize, gate_send, gate_x, cross)
             forward(gate, 3 - p, i, gsize, gate_send, gate_sa, sibling)
-            arrived(gate, 3 - pc, i, gsize, gate_x)
-            forward(gate, 3 - pc, i, gsize, gate_send, gate_sb, sibling)
+            if i >= LAG:
+                share_far(i - LAG)
+
+        for grp in DISPATCH[i + 1]:
+            dispatch(grp)
+
+    def send_down():
+        @pl.when(native)
+        def _():
+            send_own(down_hbm, down, dsize, range(DOWN_CHUNKS), down_send, down_in, cross)
+
+        @pl.when(foreign)
+        def _():
+            send_own(down_hbm, down, dsize, range(DOWN_CHUNKS), down_send, down_in, across)
 
     def from_sibling(ref, k, size, chunks, sem):
         for i in chunks:
@@ -203,10 +229,11 @@
                 a, u = a + acc[r, at], u + acc[r, up]
             hidden[r, at] = (a / (1.0 + jnp.exp(-a)) * u).astype(jnp.bfloat16)
 
-    early = 5
+    early = GATE_CHUNKS - 1
     cut = early * gsize
-    first = [(p, 0, depth), (pc, 0, cut), (3 - p, 0, cut), (3 - pc, 0, cut)]
-    last = [(k, cut, depth - cut) for k in (pc, 3 - p, 3 - pc)]
+    far = (early - LAG) * gsize
+    first = [(p, 0, depth), (pc, 0, cut), (3 - p, 0, cut), (3 - pc, 0, far)]
+    last = [(pc, cut, depth - cut), (3 - p, cut, depth - cut), (3 - pc, far, depth - far)]
     whole = [(k, 0, depth) for k in (p, pc, 3 - p, 3 - pc)]
 
     for i in range(early):
@@ -217,7 +244,7 @@
         pltpu.make_async_copy(gate_hbm.at[0], gate.at[p], own_copy.at[0]).wait()
         pltpu.make_async_copy(down_hbm.at[0], down.at[p], own_copy.at[1]).wait()
         from_sibling(gate, 3 - p, gsize, range(early), gate_sa)
-        from_sibling(gate, 3 - pc, gsize, range(early), gate_sb)
+        from_sibling(gate, 3 - pc, gsize, range(early - LAG), gate_sb)
 
     @pl.when(foreign)
     def _():
@@ -227,24 +254,23 @@
     rows_in(0)
     rows_in(1)
     gate_begin(first, slice(0, 256))
-    pass_on(early)
-    rows_in(2)
-    gate_begin(first, slice(256, 384))
-    for i in range(early + 1, GATE_CHUNKS):
+    send_down()
+
+    for i in range(early, GATE_CHUNKS):
         pass_on(i)
 
     @pl.when(native)
     def _():
-        send_own(down_hbm, down, dsize, DOWN_CHUNKS, down_send, down_in, cross)
         from_sibling(gate, 3 - p, gsize, range(early, GATE_CHUNKS), gate_sa)
-        from_sibling(gate, 3 - pc, gsize, range(early, GATE_CHUNKS), gate_sb)
-
-    @pl.when(foreign)
-    def _():
-        send_own(down_hbm, down, dsize, DOWN_CHUNKS, down_send, down_in, across)
+        from_sibling(gate, 3 - pc, gsize, range(early - LAG, GATE_CHUNKS), gate_sb)
+
+    @pl.when(foreign)
+    def _():
+        for i in range(GATE_CHUNKS - LAG, GATE_CHUNKS):
+            share_far(i)
         from_sibling(gate, pc, gsize, range(early, GATE_CHUNKS), gate_sb)
 
-    gate_finish(last, slice(0, 384), True)
+    gate_finish(last, slice(0, 256), True)
 
     def quarter(k, halves):
         for half in halves:
@@ -282,9 +308,18 @@
         from_sibling(down, p, dsize, range(DOWN_CHUNKS), down_sa)
 
     quarter(p, (0,))
+    rows_in(2)
     rows_in(3)
-    gate_finish(whole, slice(384, 512), False)
+    gate_finish(whole, slice(256, 512), False)
     quarter(p, (1,))
+
+    def pass_down(chunks):
+        for i in chunks:
+            arrived(down, 3 - p, i, dsize, down_in)
+            forward(down, 3 - p, i, dsize, down_send, down_x, cross)
+            forward(down, 3 - p, i, dsize, down_send, down_sa, sibling)
+
+    half = DOWN_CHUNKS // 2
 
     @pl.when(native)
     def _():
@@ -294,12 +329,10 @@
 
     @pl.when(foreign)
     def _():
-        for i in range(DOWN_CHUNKS):
-            arrived(down, 3 - p, i, dsize, down_in)
-            forward(down, 3 - p, i, dsize, down_send, down_x, cross)
-            forward(down, 3 - p, i, dsize, down_send, down_sa, sibling)
-
-    quarter(jnp.where(native, pc, 3 - p), (0, 1))
+        pass_down(range(half))
+        from_sibling(down, pc, dsize, range(DOWN_CHUNKS), down_sb)
+
+    quarter(pc, (0, 1))
 
     @pl.when(native)
     def _():
@@ -307,9 +340,9 @@
 
     @pl.when(foreign)
     def _():
-        from_sibling(down, pc, dsize, range(DOWN_CHUNKS), down_sb)
-
-    quarter(jnp.where(native, 3 - p, pc), (0, 1))
+        pass_down(range(half, DOWN_CHUNKS))
+
+    quarter(3 - p, (0, 1))
 
     @pl.when(foreign)
     def _():

time: 212 us -> 194 us (0.915)
  Pallas kernels: 207 us -> 189 us
    pallas_call x1, Pallas kernels: 207 us -> 189 us  [local(): pl.pallas_call(kernel, out_shape=jax.ShapeDtypeStruct((tok_rows, width),...]
where the time goes in v3:
time: 194 us
  Pallas kernels  189 us (97%)
  local copies, waits for them, and re-layouts  4.96 us (3%)
    pallas_call x1, Pallas kernels, local(): pl.pallas_call(kernel, out_shape=jax.ShapeDtypeStruct((tok_rows, width),...  189 us
    unnamed x3, local copies, waits for them, and re-layouts  4.96 us

profile of v3, /device:TPU:1, one launch (start us, length us, event | category | flops | bytes accessed | tf_op | source)
XLA Modules:
  0.0 193.8 jit_solution(1270798618072562778)
XLA Ops:
  0.0 1.4 copy.7.wts_ref
  1.4 1.4 copy.6.ids_ref
  2.8 188.8 %shard_map.55 = bf16[128,3584]{1,0:T(8,128)(2,1)} custom-call(bf16[128,3584]{1,0:T(8,128)(2,1)} %tok_ref.1, bf16[1,896,2048]{2,1,0:T(8,128)(2,1)} %gate_hbm.1, bf16[1,1024,896]{2,1,0:T(8,128)(2,1)} %down_hbm.1, s32[128,8]{1,0:T(8,128)} %copy.6.ids_ref, bf16[128,8]{1,0:T(8,128)(2,1)} %copy.7.wts_ref), custom_call_target="tpu_custom_call" | custom-call | tf_op jit(solution)/shard_map/pallas_call | solution.py:391
  191.6 2.2 %copy.9 = bf16[128,3584]{1,0:T(8,128)(2,1)} copy(bf16[128,3584]{1,0:T(8,128)(2,1)} %shard_map.55) | data formatting | bytes 1835008

commit v4 on v3

--- a/solution.py
+++ b/solution.py
@@ -84,12 +84,14 @@
     place[...] = jnp.where(chosen, 1.0, 0.0).astype(jnp.bfloat16)
     comb[...] = jnp.where(chosen, weight, 0.0).T.astype(jnp.bfloat16)
 
-    @pl.loop(0, 7)
-    def _(n):
-        at = pl.ds(pl.multiple_of(n * 512, 512), 512)
-        block = jnp.dot(place[...], tok_ref[:, at], preferred_element_type=jnp.float32)
-        outgoing[:, :, at] = block.astype(jnp.bfloat16).reshape(64, SLOTS, 512)
-
+    def pick(r0, r1):
+        @pl.loop(0, 7)
+        def _(n):
+            at = pl.ds(pl.multiple_of(n * 512, 512), 512)
+            block = jnp.dot(place[r0:r1, :], tok_ref[:, at], preferred_element_type=jnp.float32)
+            outgoing[r0 // 8 : r1 // 8, :, at] = block.astype(jnp.bfloat16).reshape((r1 - r0) // 8, SLOTS, 512)
+
+    pick(0, 128)
     pl.semaphore_wait(barrier, jnp.where(native, 96, 97))
 
     def remote(src, dst, ssem, rsem, to):
@@ -150,7 +152,9 @@
             else:
                 go()
 
-    for grp in DISPATCH[0]:
+    dispatch(0)
+    pick(128, 512)
+    for grp in DISPATCH[0][1:]:
         dispatch(grp)
 
     @pl.when(native)
@@ -307,18 +311,18 @@
     def _():
         from_sibling(down, p, dsize, range(DOWN_CHUNKS), down_sa)
 
+    def pass_down(chunks):
+        for i in chunks:
+            arrived(down, 3 - p, i, dsize, down_in)
+            forward(down, 3 - p, i, dsize, down_send, down_x, cross)
+            forward(down, 3 - p, i, dsize, down_send, down_sa, sibling)
+
     quarter(p, (0,))
     rows_in(2)
     rows_in(3)
     gate_finish(whole, slice(256, 512), False)
     quarter(p, (1,))
 
-    def pass_down(chunks):
-        for i in chunks:
-            arrived(down, 3 - p, i, dsize, down_in)
-            forward(down, 3 - p, i, dsize, down_send, down_x, cross)
-            forward(down, 3 - p, i, dsize, down_send, down_sa, sibling)
-
     half = DOWN_CHUNKS // 2
 
     @pl.when(native)
@@ -356,10 +360,10 @@
 
     quarter(3 - pc, (0, 1))
 
-    for k in range(4):
+    for k in (p, 3 - p, pc, 3 - pc):
         pltpu.make_async_copy(returned.at[k], returned.at[k], ret_recv.at[k]).wait()
         mixed = jnp.dot(comb[...], returned[k].reshape(512, cols), preferred_element_type=jnp.float32)
-        out_ref[:, k * cols : (k + 1) * cols] = mixed.astype(jnp.bfloat16)
+        out_ref[:, pl.ds(pl.multiple_of(k * cols, 128), cols)] = mixed.astype(jnp.bfloat16)
 
     def sent(ref, sem):
         pltpu.make_async_copy(ref, ref, sem).wait()

time: 194 us -> 193 us (level)
  no operation moved by 1% of the time
where the time goes in v4:
time: 193 us
  Pallas kernels  188 us (97%)
  local copies, waits for them, and re-layouts  4.96 us (3%)
    pallas_call x1, Pallas kernels, local(): pl.pallas_call(kernel, out_shape=jax.ShapeDtypeStruct((tok_rows, width),...  188 us
    unnamed x3, local copies, waits for them, and re-layouts  4.96 us

profile of v4, /device:TPU:1, one launch (start us, length us, event | category | flops | bytes accessed | tf_op | source)
XLA Modules:
  0.0 192.6 jit_solution(16577661239189901967)
XLA Ops:
  0.0 1.4 copy.7.wts_ref
  1.4 1.4 copy.6.ids_ref
  2.8 187.6 %shard_map.55 = bf16[128,3584]{1,0:T(8,128)(2,1)} custom-call(bf16[128,3584]{1,0:T(8,128)(2,1)} %tok_ref.1, bf16[1,896,2048]{2,1,0:T(8,128)(2,1)} %gate_hbm.1, bf16[1,1024,896]{2,1,0:T(8,128)(2,1)} %down_hbm.1, s32[128,8]{1,0:T(8,128)} %copy.6.ids_ref, bf16[128,8]{1,0:T(8,128)(2,1)} %copy.7.wts_ref), custom_call_target="tpu_custom_call" | custom-call | tf_op jit(solution)/shard_map/pallas_call | solution.py:395
  190.4 2.2 %copy.9 = bf16[128,3584]{1,0:T(8,128)(2,1)} copy(bf16[128,3584]{1,0:T(8,128)(2,1)} %shard_map.55) | data formatting | bytes 1835008

commit v5 on v4

--- a/solution.py
+++ b/solution.py
@@ -17,7 +17,7 @@
 DOWN_CHUNKS = 4
 AHEAD = 7
 LAG = 1
-DISPATCH = ((0,), (1,), (), (2,), (3,), (), (), ())
+DISPATCH = (16, 32, 32, 48, 64, 64, 64, 64)
 
 
 def kernel(
@@ -67,8 +67,8 @@
     dz = jnp.where(zs == 0, dz0, dz1)
     core = jnp.where(b == 0, m, 1 - m)
     expert = ((z + dz) % NZ * 4 + (x + dx) % NX) * 2 + core
-    ids = ids_ref[...].T
-    wts = wts_ref[...].astype(jnp.float32).T
+    ids = ids_ref[...]
+    wts = wts_ref[...].astype(jnp.float32)
     named = jnp.zeros((512, 128), jnp.float32)
     weight = jnp.zeros((512, 128), jnp.float32)
     for k in range(8):
@@ -126,8 +126,8 @@
 
     send_gate(range(AHEAD))
 
-    def dispatch(grp):
-        @pl.loop(0, 16)
+    def dispatch_part(grp, lo, hi):
+        @pl.loop(lo, hi)
         def _(i):
             zsel, bb, ddx = i % 2, (i // 2) % 2, i // 4
             ddz = DZ0[grp] + (DZ1[grp] - DZ0[grp]) * zsel
@@ -152,10 +152,14 @@
             else:
                 go()
 
-    dispatch(0)
+    def dispatch(lo, hi):
+        for grp in range(GROUPS):
+            if max(lo, grp * 16) < min(hi, grp * 16 + 16):
+                dispatch_part(grp, max(lo - grp * 16, 0), min(hi - grp * 16, 16))
+
+    dispatch(0, 16)
     pick(128, 512)
-    for grp in DISPATCH[0][1:]:
-        dispatch(grp)
+    dispatch(16, DISPATCH[0])
 
     @pl.when(native)
     def _():
@@ -184,8 +188,7 @@
             if i >= LAG:
                 share_far(i - LAG)
 
-        for grp in DISPATCH[i + 1]:
-            dispatch(grp)
+        dispatch(DISPATCH[i], DISPATCH[i + 1])
 
     def send_down():
         @pl.when(native)
@@ -417,7 +420,7 @@
         compiler_params=pltpu.CompilerParams(
             collective_id=0, has_side_effects=True, vmem_limit_bytes=60 * 1024 * 1024
         ),
-    )(tokens, gate_up, down_proj, expert_ids, gate_weights)
+    )(tokens, gate_up, down_proj, expert_ids.T, gate_weights.T)
 
 
 def solution(mesh):

time: 193 us -> 190 us (0.984)
  local copies, waits for them, and re-layouts: 4.96 us -> 2.16 us
    unnamed x3 -> x1, local copies, waits for them, and re-layouts: 4.96 us -> 2.16 us
where the time goes in v5:
time: 190 us
  Pallas kernels  188 us (99%)
  local copies, waits for them, and re-layouts  2.16 us (1%)
    pallas_call x1, Pallas kernels, local(): pl.pallas_call(kernel, out_shape=jax.ShapeDtypeStruct((tok_rows, width),...  188 us

profile of v5, /device:TPU:1, one launch (start us, length us, event | category | flops | bytes accessed | tf_op | source)
XLA Modules:
  0.0 189.7 jit_solution(16754969456874555371)
XLA Ops:
  0.0 187.6 %shard_map.55 = bf16[128,3584]{1,0:T(8,128)(2,1)} custom-call(bf16[128,3584]{1,0:T(8,128)(2,1)} %tok_ref.1, bf16[1,896,2048]{2,1,0:T(8,128)(2,1)} %gate_hbm.1, bf16[1,1024,896]{2,1,0:T(8,128)(2,1)} %down_hbm.1, s32[8,128]{1,0:T(8,128)} %bitcast.2, bf16[8,128]{1,0:T(8,128)(2,1)} %bitcast.3), custom_call_target="tpu_custom_call" | custom-call | tf_op jit(solution)/shard_map/pallas_call | solution.py:398
  187.6 2.2 %copy.7 = bf16[128,3584]{1,0:T(8,128)(2,1)} copy(bf16[128,3584]{1,0:T(8,128)(2,1)} %shard_map.55) | data formatting | bytes 1835008

commit v6 on v5

--- a/solution.py
+++ b/solution.py
@@ -21,10 +21,11 @@
 
 
 def kernel(
-    tok_ref, gate_hbm, down_hbm, ids_ref, wts_ref, out_ref,
+    tok_hbm, gate_hbm, down_hbm, ids_ref, wts_ref, out_ref,
     place, comb, outgoing, rows, rows2, gate, down, acc, hidden, result, returned,
     disp_send, disp_recv, own_copy, gate_send, gate_in, gate_x, gate_sa, gate_sb,
     down_send, down_in, down_x, down_sa, down_sb, ret_send, ret_recv,
+    tok_ref, tok_sem,
 ):
     p = lax.axis_index("dp")
     e = lax.axis_index("expert")
@@ -40,6 +41,9 @@
     ff = hidden.shape[1]
     depth = gate.shape[1]
     cols = down.shape[2]
+
+    tok_copy = pltpu.make_async_copy(tok_hbm, tok_ref, tok_sem)
+    tok_copy.start()
 
     barrier = pltpu.get_barrier_semaphore()
 
@@ -91,6 +95,7 @@
             block = jnp.dot(place[r0:r1, :], tok_ref[:, at], preferred_element_type=jnp.float32)
             outgoing[r0 // 8 : r1 // 8, :, at] = block.astype(jnp.bfloat16).reshape((r1 - r0) // 8, SLOTS, 512)
 
+    tok_copy.wait()
     pick(0, 128)
     pl.semaphore_wait(barrier, jnp.where(native, 96, 97))
 
@@ -398,7 +403,7 @@
     return pl.pallas_call(
         kernel,
         out_shape=jax.ShapeDtypeStruct((tok_rows, width), bf),
-        in_specs=[vmem, hbm, hbm, vmem, vmem],
+        in_specs=[hbm, hbm, hbm, vmem, vmem],
         out_specs=vmem,
         scratch_shapes=[
             pltpu.VMEM((512, 128), bf),
@@ -416,6 +421,7 @@
             dma, dma((GATE_CHUNKS,)), dma((GATE_CHUNKS,)), dma((GATE_CHUNKS,)), dma((GATE_CHUNKS,)),
             dma, dma((DOWN_CHUNKS,)), dma((DOWN_CHUNKS,)), dma((DOWN_CHUNKS,)), dma((DOWN_CHUNKS,)),
             dma, dma((4,)),
+            pltpu.VMEM((tok_rows, width), bf), dma,
         ],
         compiler_params=pltpu.CompilerParams(
             collective_id=0, has_side_effects=True, vmem_limit_bytes=60 * 1024 * 1024

time: 190 us -> 189 us (level)
  no operation moved by 1% of the time
where the time goes in v6:
time: 189 us
  Pallas kernels  187 us (99%)
  local copies, waits for them, and re-layouts  2.16 us (1%)
    pallas_call x1, Pallas kernels, local(): pl.pallas_call(kernel, out_shape=jax.ShapeDtypeStruct((tok_rows, width),...  187 us

profile of v6, /device:TPU:1, one launch (start us, length us, event | category | flops | bytes accessed | tf_op | source)
XLA Modules:
  0.0 189.1 jit_solution(7387417367731106693)
XLA Ops:
  0.0 187.0 %shard_map.55 = bf16[128,3584]{1,0:T(8,128)(2,1)} custom-call(bf16[128,3584]{1,0:T(8,128)(2,1)} %tok_hbm.1, bf16[1,896,2048]{2,1,0:T(8,128)(2,1)} %gate_hbm.1, bf16[1,1024,896]{2,1,0:T(8,128)(2,1)} %down_hbm.1, s32[8,128]{1,0:T(8,128)} %bitcast.2, bf16[8,128]{1,0:T(8,128)(2,1)} %bitcast.3), custom_call_target="tpu_custom_call" | custom-call | tf_op jit(solution)/shard_map/pallas_call | solution.py:403
  187.0 2.2 %copy.7 = bf16[128,3584]{1,0:T(8,128)(2,1)} copy(bf16[128,3584]{1,0:T(8,128)(2,1)} %shard_map.55) | data formatting | bytes 1835008
